TPU v7x, 32 devices: a whole 2x2x4 slice. The times are simulated.
32 devices in a mesh: ctx: 8 (over y, x, core), head: 4 (over z).
Axes of the slice: x: 2, y: 2, z: 4, core: 2. Of those that a mesh axis runs over, the one named last changes fastest.
Arguments:
- queries: bfloat16 [3072, 8192], P('ctx', 'head'), may hold values from -45 to 45
- keys: bfloat16 [3072, 1024], P('ctx', 'head'), may hold values from -4 to 4
- values: bfloat16 [3072, 1024], P('ctx', 'head'), may hold values from -16 to 16
- gate_mask: int32 [64], P('head'), may hold values 0 or 1
- w_out: bfloat16 [8192, 8192], P('head'), may hold values from -0.0625 to 0.0625
Outputs:
- attn_out: bfloat16 [3072, 8192], P(('ctx', 'head'))
All inputs are finite; a program needn't handle non-finite values. No bound on the sum of `gate_mask` on one device may be relied on, other than what follows from the above.
Results may differ from a plain program's by a relative error of at most 0.01.
Values may be sent and summed in bfloat16 or wider, within the bound.
A program may use at most 128 MiB of HBM per device.

v0:
```python
import jax
import jax.numpy as jnp
from jax import lax
from jax.sharding import PartitionSpec as P

HD = 128
SINK = 128
WINDOW = 256


def spread(value, axis, root):
    mine = lax.axis_index(axis) == root
    return lax.psum(jnp.where(mine, value, jnp.zeros_like(value)), axis)


def passed_along(value, axis, by):
    peers = lax.axis_size(axis)
    pairs = [(i, i + by) for i in range(peers) if 0 <= i + by < peers]
    return lax.ppermute(value, axis, pairs)


def online_update(state, segment, query_pos, key_block, value_block, key_pos):
    run_max, run_sum, run_acc = state
    scores = jnp.einsum(
        "tgrd,kgd->grtk", segment, key_block, preferred_element_type=jnp.float32
    ) * HD ** (-0.5)
    allowed = key_pos[None, :] <= query_pos[:, None]
    masked_scores = jnp.where(allowed, scores, -1e30)
    new_max = jnp.maximum(run_max, jnp.max(masked_scores, axis=-1))
    rescale = jnp.exp(run_max - new_max)
    weights = jnp.where(allowed, jnp.exp(masked_scores - new_max[..., None]), 0.0)
    new_sum = run_sum * rescale + jnp.sum(weights, axis=-1)
    new_acc = run_acc * rescale[..., None] + jnp.einsum(
        "grtk,kgd->grtd",
        weights.astype(jnp.bfloat16),
        value_block,
        preferred_element_type=jnp.float32,
    )
    return (new_max, new_sum, new_acc)


def keep_state(state):
    return state


def shards(queries, keys, values, gate_mask, w_out):
    tok_rows = queries.shape[0]
    groups_local = keys.shape[1] // HD
    heads_local = queries.shape[1] // HD
    repeats = heads_local // groups_local
    ctx_index = lax.axis_index("ctx")
    row_offset = ctx_index * tok_rows
    query_pos = row_offset + jnp.arange(tok_rows, dtype=jnp.int32)
    own_queries = queries.reshape(tok_rows, groups_local, repeats, HD)
    sink_keys, sink_values = (spread(keys[:SINK], "ctx", 0), spread(values[:SINK], "ctx", 0))
    left_keys, left_values = passed_along(
        (keys[tok_rows - WINDOW :], values[tok_rows - WINDOW :]), "ctx", 1
    )
    near_keys = jnp.concatenate([sink_keys, left_keys, keys], axis=0)
    near_values = jnp.concatenate([sink_values, left_values, values], axis=0)
    near_count = near_keys.shape[0]
    near_pos = jnp.concatenate(
        [
            jnp.arange(SINK, dtype=jnp.int32),
            row_offset - WINDOW + jnp.arange(WINDOW, dtype=jnp.int32),
            query_pos,
        ]
    )
    is_sink = jnp.arange(near_count) < SINK
    query_col = query_pos[:, None]
    key_row = near_pos[None, :]
    recent = (key_row <= query_col) & (key_row > query_col - WINDOW) & (key_row >= 0)
    allowed = jnp.where(is_sink[None, :], key_row <= query_col - WINDOW, recent)
    near_scores = jnp.einsum(
        "tgrd,kgd->grtk",
        own_queries,
        near_keys.reshape(near_count, groups_local, HD),
        preferred_element_type=jnp.float32,
    ) * HD ** (-0.5)
    masked_scores = jnp.where(allowed, near_scores, -1e30)
    row_max = jnp.max(masked_scores, axis=-1, keepdims=True)
    weights = jnp.where(allowed, jnp.exp(masked_scores - row_max), 0.0)
    weight_sum = jnp.sum(weights, axis=-1)
    stream_out = (
        jnp.einsum(
            "grtk,kgd->grtd",
            weights.astype(jnp.bfloat16),
            near_values.reshape(near_count, groups_local, HD),
            preferred_element_type=jnp.float32,
        )
        / weight_sum[..., None]
    )
    fold_queries, fold_keys, fold_values = (queries, keys, values)
    seg_starts = [row_offset]
    fold_grouped = fold_queries.reshape(tok_rows, groups_local, repeats, HD)
    segments = [fold_grouped]
    seg_positions = [first_pos + jnp.arange(tok_rows, dtype=jnp.int32) for first_pos in seg_starts]
    initial = tuple(
        (
            (
                jnp.full((groups_local, repeats, tok_rows), -1e30, jnp.float32),
                jnp.zeros((groups_local, repeats, tok_rows), jnp.float32),
                jnp.zeros((groups_local, repeats, tok_rows, HD), jnp.float32),
            )
            for first_pos in seg_starts
        )
    )

    def update_all(states_in, key_block, value_block, key_pos):
        updated = []
        for segment, seg_pos, state in zip(segments, seg_positions, states_in):

            def attend_segment(state_now, segment=segment, seg_pos=seg_pos):
                return online_update(state_now, segment, seg_pos, key_block, value_block, key_pos)

            updated.append(
                lax.cond(jnp.min(key_pos) <= seg_pos[-1], attend_segment, keep_state, state)
            )
        return tuple(updated)

    fetched_keys = lax.all_gather(fold_keys, "ctx", axis=0, tiled=True)
    fetched_values = lax.all_gather(fold_values, "ctx", axis=0, tiled=True)
    piece_rows = fetched_keys.shape[0]
    row_index = jnp.arange(piece_rows, dtype=jnp.int32)
    grouped_keys = fetched_keys.reshape(piece_rows, groups_local, HD)
    grouped_values = fetched_values.reshape(piece_rows, groups_local, HD)
    block_rows = 512

    def loop_body(block_index, states_now):
        first = block_index * block_rows
        return update_all(
            states_now,
            lax.dynamic_slice_in_dim(grouped_keys, first, block_rows, 0),
            lax.dynamic_slice_in_dim(grouped_values, first, block_rows, 0),
            lax.dynamic_slice_in_dim(row_index, first, block_rows, 0),
        )

    states = lax.fori_loop(0, piece_rows // block_rows, loop_body, initial)
    results = [(state[2] / state[1][..., None]).astype(jnp.bfloat16) for state in states]
    full_out = results[0]
    gate_on = gate_mask.reshape(groups_local, repeats)[:, :, None, None] == 1
    mixed_heads = jnp.where(gate_on, full_out, stream_out.astype(jnp.bfloat16))
    mixed_rows = jnp.transpose(mixed_heads, (2, 0, 1, 3)).reshape(tok_rows, heads_local * HD)
    partial_value = jnp.dot(mixed_rows, w_out, preferred_element_type=jnp.float32)
    summed = lax.psum_scatter(
        partial_value.astype(jnp.bfloat16), "head", scatter_dimension=0, tiled=True
    )
    return summed


def solution(mesh):
    in_specs = (P("ctx", "head"), P("ctx", "head"), P("ctx", "head"), P("head"), P("head", None))
    out_specs = P(("ctx", "head"), None)
    return jax.shard_map(shards, mesh=mesh, in_specs=in_specs, out_specs=out_specs, check_vma=False)
```

profile of v0, /device:TPU:6, one launch (start us, length us, event | category | flops | bytes accessed | tf_op | source)
XLA Modules:
  0.0 364.8 jit_solution(8275021923778631088)
XLA Ops:
  13.3 1.9 collective-permute-start
  16.8 1.9 collective-permute-start.1
  20.9 1.9 copy.12
  23.8 39.3 %all-reduce.3.cloned.1.call-done = (bf16[128,256]{0,1:T(8,128)(2,1)}, bf16[128,256]{0,1:T(8,128)(2,1)}) async-done(((bf16[128,256]{0,1:T(8,128)(2,1)}, bf16[128,256]{0,1:T(8,128)(2,1)}), (bf16[128,256]{0,1:T(8,128)(2,1)}, bf16[128,256]{0,1:T(8,128)(2,1)})) %all-reduce.3.cloned.1.call-update) | async-done | bytes 131088 | tf_op jit(solution)/shard_map/psum | solution.py:13
  64.7 1.7 pad_maximum_fusion
  66.4 1.9 copy.25
  68.3 1.7 pad_maximum_fusion.1
  70.0 12.3 %fusion.35 = (f32[2,8,384]{2,1,0:T(8,128)S(1)}, bf16[2,8,384,768]{2,3,1,0:T(8,128)(2,1)}) fusion(pred[384,768]{0,1:T(8,128)(4,1)} %and_select_fusion, bf16[768,2,128,1]{0,2,3,1:T(8,128)(2,1)} %bitcast.69, bf16[384,2,8,128]{0,3,2,1:T(8,128)(2,1)S(1)} %bitcast.65), kind=kOutput, calls=%fused_computation.50 | convolution fusion | flops 1236271872 | bytes 11722752 | tf_op jit(solution)/shard_map/sub | solution.py:82
  82.3 8.7 %all-gather.3.cloned.1.call-done = bf16[3072,256]{0,1:T(8,128)(2,1)} async-done(((bf16[384,256]{0,1:T(8,128)(2,1)}), bf16[3072,256]{0,1:T(8,128)(2,1)}) %all-gather.3.cloned.1.call-update) | async-done | bytes 1572880 | tf_op jit(solution)/shard_map/all_gather | solution.py:121
  91.1 1.9 copy.14
  93.0 26.0 %all-gather.5.cloned.1.call-done = bf16[3072,256]{0,1:T(8,128)(2,1)} async-done(((bf16[384,256]{0,1:T(8,128)(2,1)}), bf16[3072,256]{0,1:T(8,128)(2,1)}) %all-gather.5.cloned.1.call-update) | async-done | bytes 1572880 | tf_op jit(solution)/shard_map/all_gather | solution.py:122
  119.0 2.6 copy.16
  121.6 2.0 broadcast_in_dim.68
  123.6 93.7 %while.17 = (s32[]{:T(128)}, f32[2,8,384]{2,1,0:T(8,128)S(1)}, f32[2,8,384]{2,1,0:T(8,128)S(1)}, f32[2,8,384,128]{3,2,1,0:T(8,128)}, s32[3072]{0:T(1024)S(1)}, /...) while((s32[]{:T(128)}, f32[2,8,384]{2,1,0:T(8,128)S(1)}, ...), condition=%wide.region_6.7_spmd, body=%wide.region_0.6_spmd.sunk | while | flops 1653289472 | bytes 72491400 | solution.py:138
  126.3 12.9 %conditional.2 = ((f32[2,8,384]{2,1,0:T(8,128)S(1)}, f32[2,8,384]{2,1,0:T(8,128)S(1)}, f32[2,8,384,128]{3,2,1,0:T(8,128)})) conditional(s32[]{:T(128)} %convert_element_type.46, (f32[2,8,384]{2,1,0:T(8,128)S(1)}, f32[2,8,384]{2,1,0:T(8,128)S(1)}, f32[2,8,384,128]{3,2,1,0:T(8,128)}) %tuple.50, (s32[512]{0:T(512)S(1)}, s32[384]{0:T(512)S(1)}, ...), branch_computations={%region_2.2_spmd, %region_3.5_spmd} | conditional | flops 1653288960 | bytes 72487000 | solution.py:117
  126.5 2.0 fusion
  128.6 3.0 fusion.2
  131.6 5.9 %multiply_add_fusion = f32[2,8,384,128]{3,2,1,0:T(8,128)S(1)} fusion(f32[2,8,384,128]{3,2,1,0:T(8,128)S(1)} %copy-done, f32[2,512,384,8]{2,1,3,0:T(8,128)S(1)} %get-tuple-element.283, f32[2,8,384]{2,1,0:T(8,128)S(1)} %max.4, pred[384,512]{0,1:T(8,128)(4,1)S(1)} %broadcast_compare_fusion, f32[2,8,384]{2,1,0:T(8,128)S(1)} %get-tuple-element.279, ...), kind=kOutput, calls=%fused_computation.7 | convolution fusion | flops 822607872 | bytes 19382784 | tf_op jit(solution)/shard_map/while/body/eval_jaxpr/cond/branch_1_fun/grtk,kgd->grtd/dot_general | solution.py:33
  137.5 1.6 copy-done.1
  141.9 12.9 %conditional.2 = ((f32[2,8,384]{2,1,0:T(8,128)S(1)}, f32[2,8,384]{2,1,0:T(8,128)S(1)}, f32[2,8,384,128]{3,2,1,0:T(8,128)})) conditional(s32[]{:T(128)} %convert_element_type.46, (f32[2,8,384]{2,1,0:T(8,128)S(1)}, f32[2,8,384]{2,1,0:T(8,128)S(1)}, f32[2,8,384,128]{3,2,1,0:T(8,128)}) %tuple.50, (s32[512]{0:T(512)S(1)}, s32[384]{0:T(512)S(1)}, ...), branch_computations={%region_2.2_spmd, %region_3.5_spmd} | conditional | flops 1653288960 | bytes 72487000 | solution.py:117
  142.1 2.0 fusion
  144.2 3.0 fusion.2
  147.2 5.9 %multiply_add_fusion = f32[2,8,384,128]{3,2,1,0:T(8,128)S(1)} fusion(f32[2,8,384,128]{3,2,1,0:T(8,128)S(1)} %copy-done, f32[2,512,384,8]{2,1,3,0:T(8,128)S(1)} %get-tuple-element.283, f32[2,8,384]{2,1,0:T(8,128)S(1)} %max.4, pred[384,512]{0,1:T(8,128)(4,1)S(1)} %broadcast_compare_fusion, f32[2,8,384]{2,1,0:T(8,128)S(1)} %get-tuple-element.279, ...), kind=kOutput, calls=%fused_computation.7 | convolution fusion | flops 822607872 | bytes 19382784 | tf_op jit(solution)/shard_map/while/body/eval_jaxpr/cond/branch_1_fun/grtk,kgd->grtd/dot_general | solution.py:33
  153.2 1.6 copy-done.1
  157.5 12.9 %conditional.2 = ((f32[2,8,384]{2,1,0:T(8,128)S(1)}, f32[2,8,384]{2,1,0:T(8,128)S(1)}, f32[2,8,384,128]{3,2,1,0:T(8,128)})) conditional(s32[]{:T(128)} %convert_element_type.46, (f32[2,8,384]{2,1,0:T(8,128)S(1)}, f32[2,8,384]{2,1,0:T(8,128)S(1)}, f32[2,8,384,128]{3,2,1,0:T(8,128)}) %tuple.50, (s32[512]{0:T(512)S(1)}, s32[384]{0:T(512)S(1)}, ...), branch_computations={%region_2.2_spmd, %region_3.5_spmd} | conditional | flops 1653288960 | bytes 72487000 | solution.py:117
  157.7 2.0 fusion
  159.8 3.0 fusion.2
  162.8 5.9 %multiply_add_fusion = f32[2,8,384,128]{3,2,1,0:T(8,128)S(1)} fusion(f32[2,8,384,128]{3,2,1,0:T(8,128)S(1)} %copy-done, f32[2,512,384,8]{2,1,3,0:T(8,128)S(1)} %get-tuple-element.283, f32[2,8,384]{2,1,0:T(8,128)S(1)} %max.4, pred[384,512]{0,1:T(8,128)(4,1)S(1)} %broadcast_compare_fusion, f32[2,8,384]{2,1,0:T(8,128)S(1)} %get-tuple-element.279, ...), kind=kOutput, calls=%fused_computation.7 | convolution fusion | flops 822607872 | bytes 19382784 | tf_op jit(solution)/shard_map/while/body/eval_jaxpr/cond/branch_1_fun/grtk,kgd->grtd/dot_general | solution.py:33
  168.8 1.6 copy-done.1
  173.1 12.9 %conditional.2 = ((f32[2,8,384]{2,1,0:T(8,128)S(1)}, f32[2,8,384]{2,1,0:T(8,128)S(1)}, f32[2,8,384,128]{3,2,1,0:T(8,128)})) conditional(s32[]{:T(128)} %convert_element_type.46, (f32[2,8,384]{2,1,0:T(8,128)S(1)}, f32[2,8,384]{2,1,0:T(8,128)S(1)}, f32[2,8,384,128]{3,2,1,0:T(8,128)}) %tuple.50, (s32[512]{0:T(512)S(1)}, s32[384]{0:T(512)S(1)}, ...), branch_computations={%region_2.2_spmd, %region_3.5_spmd} | conditional | flops 1653288960 | bytes 72487000 | solution.py:117
  173.3 2.0 fusion
  175.4 3.0 fusion.2
  178.5 5.9 %multiply_add_fusion = f32[2,8,384,128]{3,2,1,0:T(8,128)S(1)} fusion(f32[2,8,384,128]{3,2,1,0:T(8,128)S(1)} %copy-done, f32[2,512,384,8]{2,1,3,0:T(8,128)S(1)} %get-tuple-element.283, f32[2,8,384]{2,1,0:T(8,128)S(1)} %max.4, pred[384,512]{0,1:T(8,128)(4,1)S(1)} %broadcast_compare_fusion, f32[2,8,384]{2,1,0:T(8,128)S(1)} %get-tuple-element.279, ...), kind=kOutput, calls=%fused_computation.7 | convolution fusion | flops 822607872 | bytes 19382784 | tf_op jit(solution)/shard_map/while/body/eval_jaxpr/cond/branch_1_fun/grtk,kgd->grtd/dot_general | solution.py:33
  184.4 1.6 copy-done.1
  188.8 12.9 %conditional.2 = ((f32[2,8,384]{2,1,0:T(8,128)S(1)}, f32[2,8,384]{2,1,0:T(8,128)S(1)}, f32[2,8,384,128]{3,2,1,0:T(8,128)})) conditional(s32[]{:T(128)} %convert_element_type.46, (f32[2,8,384]{2,1,0:T(8,128)S(1)}, f32[2,8,384]{2,1,0:T(8,128)S(1)}, f32[2,8,384,128]{3,2,1,0:T(8,128)}) %tuple.50, (s32[512]{0:T(512)S(1)}, s32[384]{0:T(512)S(1)}, ...), branch_computations={%region_2.2_spmd, %region_3.5_spmd} | conditional | flops 1653288960 | bytes 72487000 | solution.py:117
  189.0 2.0 fusion
  191.0 3.0 fusion.2
  194.1 5.9 %multiply_add_fusion = f32[2,8,384,128]{3,2,1,0:T(8,128)S(1)} fusion(f32[2,8,384,128]{3,2,1,0:T(8,128)S(1)} %copy-done, f32[2,512,384,8]{2,1,3,0:T(8,128)S(1)} %get-tuple-element.283, f32[2,8,384]{2,1,0:T(8,128)S(1)} %max.4, pred[384,512]{0,1:T(8,128)(4,1)S(1)} %broadcast_compare_fusion, f32[2,8,384]{2,1,0:T(8,128)S(1)} %get-tuple-element.279, ...), kind=kOutput, calls=%fused_computation.7 | convolution fusion | flops 822607872 | bytes 19382784 | tf_op jit(solution)/shard_map/while/body/eval_jaxpr/cond/branch_1_fun/grtk,kgd->grtd/dot_general | solution.py:33
  200.0 1.6 copy-done.1
  204.4 12.9 %conditional.2 = ((f32[2,8,384]{2,1,0:T(8,128)S(1)}, f32[2,8,384]{2,1,0:T(8,128)S(1)}, f32[2,8,384,128]{3,2,1,0:T(8,128)})) conditional(s32[]{:T(128)} %convert_element_type.46, (f32[2,8,384]{2,1,0:T(8,128)S(1)}, f32[2,8,384]{2,1,0:T(8,128)S(1)}, f32[2,8,384,128]{3,2,1,0:T(8,128)}) %tuple.50, (s32[512]{0:T(512)S(1)}, s32[384]{0:T(512)S(1)}, ...), branch_computations={%region_2.2_spmd, %region_3.5_spmd} | conditional | flops 1653288960 | bytes 72487000 | solution.py:117
  204.6 2.0 fusion
  206.6 3.0 fusion.2
  209.7 5.9 %multiply_add_fusion = f32[2,8,384,128]{3,2,1,0:T(8,128)S(1)} fusion(f32[2,8,384,128]{3,2,1,0:T(8,128)S(1)} %copy-done, f32[2,512,384,8]{2,1,3,0:T(8,128)S(1)} %get-tuple-element.283, f32[2,8,384]{2,1,0:T(8,128)S(1)} %max.4, pred[384,512]{0,1:T(8,128)(4,1)S(1)} %broadcast_compare_fusion, f32[2,8,384]{2,1,0:T(8,128)S(1)} %get-tuple-element.279, ...), kind=kOutput, calls=%fused_computation.7 | convolution fusion | flops 822607872 | bytes 19382784 | tf_op jit(solution)/shard_map/while/body/eval_jaxpr/cond/branch_1_fun/grtk,kgd->grtd/dot_general | solution.py:33
  215.6 1.6 copy-done.1
  217.3 2.4 copy.17
  219.6 5.3 %fusion.29 = bf16[2,8,384,128]{2,3,1,0:T(8,128)(2,1)S(1)} fusion(f32[2,8,384,128]{2,3,1,0:T(8,128)S(1)} %copy.17, f32[2,8,384]{2,1,0:T(8,128)S(1)} %get-tuple-element.248, pred[2,8]{1,0:T(4,128)(4,1)S(1)} %eq.16, f32[2,8,384]{2,1,0:T(8,128)S(1)} %get-tuple-element.284, bf16[768,2,128,1]{0,2,3,1:T(8,128)(2,1)} %bitcast.68, ...), kind=kOutput, calls=%fused_computation.34 | convolution fusion | flops 1211891712 | bytes 14598160 | tf_op jit(solution)/shard_map/grtk,kgd->grtd/dot_general | solution.py:85
  224.9 21.5 %convolution_convert_fusion = bf16[384,8192]{1,0:T(8,128)(2,1)} fusion(bf16[384,2048]{0,1:T(8,128)(2,1)S(1)} %bitcast.70, bf16[2048,8192]{1,0:T(8,128)(2,1)} %param.13), kind=kOutput, calls=%fused_computation.25 | convolution fusion | flops 12888047616 | bytes 41418752 | tf_op jit(solution)/shard_map/dot_general | solution.py:144
  246.4 111.8 %reduce-scatter.2.cloned.1.call-done = bf16[96,8192]{1,0:T(8,128)(2,1)} async-done(((bf16[384,8192]{1,0:T(8,128)(2,1)}), bf16[96,8192]{1,0:T(8,128)(2,1)}) %reduce-scatter.2.cloned.1.call-update) | async-done | bytes 1572880 | tf_op jit(solution)/shard_map/reduce_scatter | solution.py:145
  (92 shorter events, 22.7 us)
Async XLA Ops:
  6.5 58.2 %copy-start.4 = (bf16[384,256]{1,0:T(8,128)(2,1)S(1)}, bf16[384,256]{1,0:T(8,128)(2,1)}, u32[]{:S(2)}) copy-start(bf16[384,256]{1,0:T(8,128)(2,1)} %param.11) | copy-start | bytes 589828
  6.5 56.6 %all-reduce.3.cloned.1.call-start = ((), (), s32[]{:S(2)}) async-start(), calls=%async_computation.4 | async-start | bytes 262144 | tf_op jit(solution)/shard_map/psum | solution.py:13
  7.7 2.6 copy-start.2
  8.8 2.2 copy-start.5
  10.2 80.8 %all-gather.3.cloned.1.call-start = ((), (), s32[]{:S(2)}) async-start(), calls=%async_computation.1 | async-start | bytes 1769472 | tf_op jit(solution)/shard_map/all_gather | solution.py:121
  11.0 57.4 %copy-start.3 = (bf16[384,256]{0,1:T(8,128)(2,1)S(1)}, bf16[384,256]{0,1:T(8,128)(2,1)}, u32[]{:S(2)}) copy-start(bf16[384,256]{0,1:T(8,128)(2,1)} %copy-done.2) | copy-start | bytes 589828
  11.0 108.0 %all-gather.5.cloned.1.call-start = ((), (), s32[]{:S(2)}) async-start(), calls=%async_computation.2 | async-start | bytes 1769472 | tf_op jit(solution)/shard_map/all_gather | solution.py:122
  11.7 346.5 %reduce-scatter.2.cloned.1.call-start = ((), (), s32[]{:S(2)}) async-start(), calls=%async_computation.3 | async-start | bytes 7864320 | tf_op jit(solution)/shard_map/reduce_scatter | solution.py:145
  13.3 55.0 %collective-permute-start = (bf16[256,256]{0,1:T(8,128)(2,1)}, bf16[256,256]{0,1:T(8,128)(2,1)}, u32[]{:S(2)}, u32[]{:S(2)}) collective-permute-start(bf16[256,256]{0,1:T(8,128)(2,1)} %slice.25), channel_id=1, source_target_pairs={{0,4},{4,8},{8,12},{12,16},{16,20},{20,24},{24,28},{1,5},{5,9},{9,... | collective-permute-start | bytes 393224 | tf_op jit(solution)/shard_map/ppermute | solution.py:19
  16.8 47.9 %collective-permute-start.1 = (bf16[256,256]{1,0:T(8,128)(2,1)}, bf16[256,256]{1,0:T(8,128)(2,1)}, u32[]{:S(2)}, u32[]{:S(2)}) collective-permute-start(bf16[256,256]{1,0:T(8,128)(2,1)} %slice.22), channel_id=1, source_target_pairs={{0,4},{4,8},{8,12},{12,16},{16,20},{20,24},{24,28},{1,5},{5,9},{9,... | collective-permute-start | bytes 393224 | tf_op jit(solution)/shard_map/ppermute | solution.py:19
  128.6 3.1 copy-start
  137.5 1.7 copy-start.1
  144.2 3.1 copy-start
  153.1 1.7 copy-start.1
  159.8 3.1 copy-start
  168.8 1.7 copy-start.1
  175.4 3.1 copy-start
  184.4 1.7 copy-start.1
  191.0 3.1 copy-start
  200.0 1.7 copy-start.1
  206.6 3.1 copy-start
  215.6 1.7 copy-start.1
Sparse Core Ops, SparseCore 0:
  10.4 52.6 all-reduce.2
  65.2 25.8 all-gather.2
  93.1 25.8 all-gather.4
  246.6 111.6 reduce-scatter.1
where the time goes:
time: 367 us; the launch traced here: 365 us
  waiting for transfers between devices  187 us (51%)
  matrix products  86.7 us (24%)
  local copies, waits for them, and re-layouts  34.5 us (9%)
  other arithmetic  30.6 us (8%)
  between operations  13.3 us (4%)
  loops' own time  8.47 us (2%)
  starting transfers between devices  3.94 us (1%)
    reduce_scatter x1, waiting for transfers between devices, shards(): lax.psum_scatter(partial_value.astype(jnp.bfloat16), 'head', scatter_dime...  112 us
    psum x1, waiting for transfers between devices, spread(): return lax.psum(jnp.where(mine, value, jnp.zeros_like(value)), axis)  39.3 us
    dot_general x6, matrix products, online_update(): jnp.einsum('grtk,kgd->grtd', weights.astype(jnp.bfloat16), value_block, p...  35.4 us
    all_gather x1, waiting for transfers between devices, shards(): fetched_values = lax.all_gather(fold_values, 'ctx', axis=0, tiled=True)  26 us
    dot_general x1, matrix products, shards(): jnp.dot(mixed_rows, w_out, preferred_element_type=jnp.float32)  21.5 us
    reduce_sum x6, other arithmetic, online_update(): new_sum = run_sum * rescale + jnp.sum(weights, axis=-1)  18 us
    sub x1, matrix products, shards(): weights = jnp.where(allowed, jnp.exp(masked_scores - row_max), 0.0)  12.3 us
    dot_general x6, matrix products, online_update(): jnp.einsum('tgrd,kgd->grtk', segment, key_block, preferred_element_type=j...  12.2 us
  transfers between devices with their start and end apart: 6, of which 4 were waited for; matrix products, arithmetic and copies ran while one was open for 8% of the time, Pallas kernels for 0%

commit v1 on v0

v1 whole, which is shorter than its diff:
```python
import functools

import jax
import jax.numpy as jnp
from jax import lax
from jax.experimental import pallas as pl
from jax.experimental.pallas import tpu as pltpu
from jax.sharding import PartitionSpec as P

HD = 128
SINK = 128
WINDOW = 256
NEG = -1e30
LOG2E = 1.4426950408889634
MESH = pl.DeviceIdType.MESH


def chunk_order(peers):
    return [sorted(range(peers), key=lambda r: (-abs(r - z), -r if z < peers / 2 else r)) for z in range(peers)]


def pick(table, row, step):
    value = jnp.int32(0)
    for z, entries in enumerate(table):
        for s, entry in enumerate(entries):
            value = value + jnp.where((row == z) & (step == s), entry, 0)
    return value


def kernel(
    C, H, G, R, T, NP, D,
    gate_ref, q_ref, k_ref, v_ref, w_ref, out_ref,
    kv, w, part, ng_ref, m_ref, l_ref, acc_ref, mixed, tmp,
    w_sem, k_recv, k_send, k_fwd, p_send, p_recv,
):
    c = lax.axis_index("ctx")
    z = lax.axis_index("head")
    p, k = c // 2, c % 2
    sibling = 2 * p + 1 - k
    chips = C // 2
    rows = T // H
    cols = D // NP

    def w_copy(n):
        return pltpu.make_async_copy(w_ref.at[:, pl.ds(n * cols, cols)], w.at[n], w_sem.at[n])

    for n in range(NP):
        w_copy(n).start()

    for g in range(G):
        kv[c, 0, g] = k_ref[:, g * HD : (g + 1) * HD]
        kv[c, 1, g] = v_ref[:, g * HD : (g + 1) * HD]

    barrier = pltpu.get_barrier_semaphore()
    for q in range(chips):
        @pl.when(q != p)
        def _():
            pl.semaphore_signal(barrier, inc=1, device_id={"ctx": 2 * q + k}, device_id_type=MESH)
    pl.semaphore_signal(barrier, inc=1, device_id={"ctx": sibling}, device_id_type=MESH)

    @pl.when(z > 0)
    def _():
        pl.semaphore_signal(barrier, inc=1, device_id={"head": z - 1}, device_id_type=MESH)

    @pl.when(z < H - 1)
    def _():
        pl.semaphore_signal(barrier, inc=1, device_id={"head": z + 1}, device_id_type=MESH)

    greeted = chips + jnp.where(z > 0, 1, 0) + jnp.where(z < H - 1, 1, 0)
    pl.semaphore_wait(barrier, greeted)

    def kv_copy(block, send, target):
        return pltpu.make_async_remote_copy(
            src_ref=kv.at[block], dst_ref=kv.at[block], send_sem=send, recv_sem=k_recv.at[block],
            device_id={"ctx": target}, device_id_type=MESH,
        )

    for q in reversed(range(chips)):
        @pl.when(q > p)
        def _():
            kv_copy(c, k_send.at[q], 2 * q + k).start()

    @pl.when(k == 0)
    def _():
        kv_copy(c, k_send.at[p], sibling).start()

    for h in range(G * R):
        off = jnp.where(gate_ref[h] == 1, 0.0, 1.0)
        ng_ref[h] = jnp.full((rows, HD), off, jnp.float32)

    scale = HD ** -0.5 * LOG2E

    def attend(g, r, b, kind):
        start = pl.multiple_of(r * rows, rows)
        q = jnp.concatenate(
            [q_ref[pl.ds(start, rows), (g * R + h) * HD : (g * R + h + 1) * HD] for h in range(R)], axis=0
        )
        s = lax.dot_general(
            q, kv[b, 0, g], (((1,), (1,)), ((), ())), preferred_element_type=jnp.float32
        ).reshape(R, rows, T)
        off = ng_ref[g * R : (g + 1) * R, :, 0:1]
        if kind != "middle":
            key_col = lax.broadcasted_iota(jnp.int32, (rows, T), 1)
            ahead = (c - b) * T + start + lax.broadcasted_iota(jnp.int32, (rows, T), 0) - key_col
            near = (ahead < WINDOW) | (b * T + key_col < SINK)
            full_bias = jnp.where(ahead >= 0, 0.0, NEG)
            stream_bias = jnp.where(near, 0.0, NEG) + full_bias
            s = s + jnp.where(off > 0.5, stream_bias[None], full_bias[None])
            top = jnp.max(s, axis=-1, keepdims=True)
            shift = 0.0
        else:
            shift = off * -NEG
            top = jnp.max(s, axis=-1, keepdims=True) - shift
        if kind == "own":
            new = top
        else:
            old = m_ref[g, :, :, 0:1]
            new = jnp.maximum(old, top)
            alpha = jnp.exp2((old - new) * scale)
        e = jnp.exp2(s * scale - (new * scale + shift))
        total = e[:, :, 0:HD]
        for i in range(1, T // HD):
            total = total + e[:, :, i * HD : (i + 1) * HD]
        pv = jnp.dot(
            e.reshape(R * rows, T).astype(jnp.bfloat16), kv[b, 1, g], preferred_element_type=jnp.float32
        ).reshape(R, rows, HD)
        m_ref[g] = jnp.broadcast_to(new, (R, rows, HD))
        if kind == "own":
            l_ref[g] = total
            acc_ref[g] = pv
        else:
            l_ref[g] = l_ref[g] * alpha + total
            acc_ref[g] = acc_ref[g] * alpha + pv

    table = chunk_order(H)

    def part_copy(r, n):
        target = jnp.where(r > z, z + 1, z - 1)
        slot = jnp.where(r == z - 1, H, r)
        return pltpu.make_async_remote_copy(
            src_ref=part.at[r, n], dst_ref=part.at[slot, n],
            send_sem=p_send.at[r, n], recv_sem=p_recv.at[slot, n],
            device_id={"head": target}, device_id_type=MESH,
        )

    def part_wait(slot, n):
        pltpu.make_async_remote_copy(
            src_ref=part.at[slot, n], dst_ref=part.at[slot, n],
            send_sem=p_send.at[0, n], recv_sem=p_recv.at[slot, n],
            device_id={"ctx": sibling}, device_id_type=MESH,
        ).wait_recv()

    def chunk(step, carry):
        r = pick(table, z, step)
        for g in range(G):
            attend(g, r, c, "own")

        def one_block(j, inner):
            rest = j - k
            odd = rest % 2
            lead = (k == 1) & (j == 0)
            b = jnp.where(lead, c - 1, 2 * (p - 1 - rest // 2) + jnp.where(odd == 0, k, 1 - k))
            b = jnp.where(b < 0, 0, b)

            @pl.when(step == 0)
            def _():
                kv_copy(b, k_send.at[0], sibling).wait_recv()

                @pl.when(jnp.logical_not(lead) & (odd == 0))
                def _():
                    kv_copy(b, k_fwd.at[b // 2], sibling).start()

            edge = (b == c - 1) | (b == 0)

            @pl.when(edge)
            def _():
                for g in range(G):
                    attend(g, r, b, "edge")

            @pl.when(jnp.logical_not(edge))
            def _():
                for g in range(G):
                    attend(g, r, b, "middle")

            return inner

        lax.fori_loop(0, c, one_block, 0)
        for g in range(G):
            o = acc_ref[g] / jnp.sum(l_ref[g], axis=-1, keepdims=True)
            for h in range(R):
                mixed[:, (g * R + h) * HD : (g * R + h + 1) * HD] = o[h].astype(jnp.bfloat16)

        has_a = ((r > z) & (z > 0)) | ((r < z) & (z < H - 1)) | ((r == z) & (z > 0))
        has_b = (r == z) & (z < H - 1)

        def piece(n, inner):
            @pl.when(step == 0)
            def _():
                w_copy(n).wait()

            tmp[...] = jnp.dot(mixed[...], w[n], preferred_element_type=jnp.float32)

            @pl.when(has_a)
            def _():
                part_wait(r, n)
                tmp[...] += part[r, n].astype(jnp.float32)

            @pl.when(has_b)
            def _():
                part_wait(H, n)
                tmp[...] += part[H, n].astype(jnp.float32)

            @pl.when(r == z)
            def _():
                out_ref[:, pl.ds(pl.multiple_of(n * cols, cols), cols)] = tmp[...].astype(jnp.bfloat16)

            @pl.when(r != z)
            def _():
                part[r, n] = tmp[...].astype(jnp.bfloat16)
                part_copy(r, n).start()

            return inner

        lax.fori_loop(0, NP, piece, 0)
        return carry

    lax.fori_loop(0, H, chunk, 0)

    for q in range(chips):
        @pl.when(q > p)
        def _():
            kv_copy(c, k_send.at[q], 2 * q + k).wait_send()

        @pl.when(q < p)
        def _():
            kv_copy(2 * q + k, k_fwd.at[q], sibling).wait_send()

    @pl.when(k == 0)
    def _():
        kv_copy(c, k_send.at[p], sibling).wait_send()

    def drain(i, carry):
        @pl.when(i // NP != z)
        def _():
            part_copy(i // NP, i % NP).wait_send()

        return carry

    lax.fori_loop(0, H * NP, drain, 0)


def solution(mesh):
    C, H = mesh.shape["ctx"], mesh.shape["head"]

    def shards(queries, keys, values, gate_mask, w_out):
        T = queries.shape[0]
        G = keys.shape[1] // HD
        R = queries.shape[1] // keys.shape[1]
        K, D = w_out.shape
        rows = T // H
        NP = 8
        vmem = pl.BlockSpec(memory_space=pltpu.VMEM)
        return pl.pallas_call(
            functools.partial(kernel, C, H, G, R, T, NP, D),
            out_shape=jax.ShapeDtypeStruct((rows, D), jnp.bfloat16),
            in_specs=[pl.BlockSpec(memory_space=pltpu.SMEM), vmem, vmem, vmem, pl.BlockSpec(memory_space=pl.ANY)],
            out_specs=vmem,
            scratch_shapes=[
                pltpu.VMEM((C, 2, G, T, HD), jnp.bfloat16),
                pltpu.VMEM((NP, K, D // NP), jnp.bfloat16),
                pltpu.VMEM((H + 1, NP, rows, D // NP), jnp.bfloat16),
                pltpu.VMEM((G * R, rows, HD), jnp.float32),
                pltpu.VMEM((G, R, rows, HD), jnp.float32),
                pltpu.VMEM((G, R, rows, HD), jnp.float32),
                pltpu.VMEM((G, R, rows, HD), jnp.float32),
                pltpu.VMEM((rows, K), jnp.bfloat16),
                pltpu.VMEM((rows, D // NP), jnp.float32),
                pltpu.SemaphoreType.DMA((NP,)),
                pltpu.SemaphoreType.DMA((C,)),
                pltpu.SemaphoreType.DMA((C // 2,)),
                pltpu.SemaphoreType.DMA((C // 2,)),
                pltpu.SemaphoreType.DMA((H, NP)),
                pltpu.SemaphoreType.DMA((H + 1, NP)),
            ],
            compiler_params=pltpu.CompilerParams(
                collective_id=0, has_side_effects=True, vmem_limit_bytes=60 * 2**20
            ),
        )(gate_mask, queries, keys, values, w_out)

    in_specs = (P("ctx", "head"), P("ctx", "head"), P("ctx", "head"), P("head"), P("head", None))
    out_specs = P(("ctx", "head"), None)
    return jax.shard_map(shards, mesh=mesh, in_specs=in_specs, out_specs=out_specs, check_vma=False)
```

time: 367 us -> 164 us (0.45)
  waiting for transfers between devices: 187 us -> 0 us
  Pallas kernels: 0 us -> 161 us
  matrix products: 86.7 us -> 0 us
  local copies, waits for them, and re-layouts: 34.5 us -> 2.65 us
  other arithmetic: 30.6 us -> 0 us
  between operations: 13.3 us -> 0.01 us
  loops' own time: 8.47 us -> 0 us
  starting transfers between devices: 3.94 us -> 0 us
    pallas_call x0 -> x1, Pallas kernels: none -> 161 us  [shards(): pl.pallas_call(functools.partial(kernel, C, H, G, R, T, NP, D), out_shape...]
    reduce_scatter x1 -> x0, waiting for transfers between devices: 112 us -> none  [shards(): lax.psum_scatter(partial_value.astype(jnp.bfloat16), 'head', scatter_dime...]
    dot_general x14 -> x0, matrix products: 74.4 us -> none  [the longest x6 35.4 us: online_update(): jnp.einsum('grtk,kgd->grtd', weights.astype(jnp.bfloat16), value_block, p...]
    psum x1 -> x0, waiting for transfers between devices: 39.3 us -> none  [spread(): return lax.psum(jnp.where(mine, value, jnp.zeros_like(value)), axis)]
    all_gather x2 -> x0, waiting for transfers between devices: 34.8 us -> none  [the longest x1 26 us: shards(): fetched_values = lax.all_gather(fold_values, 'ctx', axis=0, tiled=True)]
    reduce_sum x6 -> x0, other arithmetic: 18 us -> none  [online_update(): new_sum = run_sum * rescale + jnp.sum(weights, axis=-1)]
    sub x1 -> x0, matrix products: 12.3 us -> none  [shards(): weights = jnp.where(allowed, jnp.exp(masked_scores - row_max), 0.0)]
    cond x30 -> x0, local copies, waits for them, and re-layouts: 9.94 us -> none
  transfers between devices with their start and end apart: 6 -> 0, of which waited for: 4 -> 0; matrix products, arithmetic and copies ran while one was open for 8% -> 0% of each run, Pallas kernels for 0% -> 0%
where the time goes in v1:
time: 164 us; the launch traced here: 163 us
  Pallas kernels  161 us (98%)
  local copies, waits for them, and re-layouts  2.65 us (2%)
    pallas_call x1, Pallas kernels, shards(): pl.pallas_call(functools.partial(kernel, C, H, G, R, T, NP, D), out_shape...  161 us

profile of v1, /device:TPU:6, one launch (start us, length us, event | category | flops | bytes accessed | tf_op | source)
XLA Modules:
  0.0 163.5 jit_solution(6392039942344481530)
XLA Ops:
  0.0 160.8 %shard_map.55 = bf16[96,8192]{1,0:T(8,128)(2,1)} custom-call(s32[16]{0:T(128)} %gate_ref.1, bf16[384,2048]{1,0:T(8,128)(2,1)} %q_ref.1, bf16[384,256]{1,0:T(8,128)(2,1)} %k_ref.1, bf16[384,256]{1,0:T(8,128)(2,1)} %v_ref.1, bf16[2048,8192]{1,0:T(8,128)(2,1)} %w_ref.1), custom_call_target="tpu_custom_call" | custom-call | tf_op jit(solution)/shard_map/pallas_call | solution.py:263
  160.8 2.7 %copy.7 = bf16[96,8192]{1,0:T(8,128)(2,1)} copy(bf16[96,8192]{1,0:T(8,128)(2,1)} %shard_map.55) | data formatting | bytes 3145728

commit v2 on v1

--- a/solution.py
+++ b/solution.py
@@ -44,9 +44,6 @@
     def w_copy(n):
         return pltpu.make_async_copy(w_ref.at[:, pl.ds(n * cols, cols)], w.at[n], w_sem.at[n])
 
-    for n in range(NP):
-        w_copy(n).start()
-
     for g in range(G):
         kv[c, 0, g] = k_ref[:, g * HD : (g + 1) * HD]
         kv[c, 1, g] = v_ref[:, g * HD : (g + 1) * HD]
@@ -84,8 +81,11 @@
     def _():
         kv_copy(c, k_send.at[p], sibling).start()
 
+    for n in range(NP):
+        w_copy(n).start()
+
     for h in range(G * R):
-        off = jnp.where(gate_ref[h] == 1, 0.0, 1.0)
+        off = jnp.where(gate_ref[h] == 1, 0.0, NEG)
         ng_ref[h] = jnp.full((rows, HD), off, jnp.float32)
 
     scale = HD ** -0.5 * LOG2E
@@ -98,33 +98,39 @@
         s = lax.dot_general(
             q, kv[b, 0, g], (((1,), (1,)), ((), ())), preferred_element_type=jnp.float32
         ).reshape(R, rows, T)
-        off = ng_ref[g * R : (g + 1) * R, :, 0:1]
+        tiles = [s[:, :, i * HD : (i + 1) * HD] for i in range(T // HD)]
+        off = ng_ref[g * R : (g + 1) * R]
         if kind != "middle":
-            key_col = lax.broadcasted_iota(jnp.int32, (rows, T), 1)
-            ahead = (c - b) * T + start + lax.broadcasted_iota(jnp.int32, (rows, T), 0) - key_col
-            near = (ahead < WINDOW) | (b * T + key_col < SINK)
-            full_bias = jnp.where(ahead >= 0, 0.0, NEG)
-            stream_bias = jnp.where(near, 0.0, NEG) + full_bias
-            s = s + jnp.where(off > 0.5, stream_bias[None], full_bias[None])
-            top = jnp.max(s, axis=-1, keepdims=True)
-            shift = 0.0
-        else:
-            shift = off * -NEG
-            top = jnp.max(s, axis=-1, keepdims=True) - shift
+            row_pos = (c - b) * T + start + lax.broadcasted_iota(jnp.int32, (rows, HD), 0)
+            for i in range(T // HD):
+                key_col = i * HD + lax.broadcasted_iota(jnp.int32, (rows, HD), 1)
+                ahead = row_pos - key_col
+                near = (ahead < WINDOW) | (b * T + key_col < SINK)
+                tiles[i] = tiles[i] + jnp.maximum(jnp.where(near, 0.0, NEG)[None], off)
+                if kind == "own":
+                    tiles[i] = tiles[i] + jnp.where(ahead >= 0, 0.0, NEG)[None]
+        top = tiles[0]
+        for tile in tiles[1:]:
+            top = jnp.maximum(top, tile)
+        top = jnp.broadcast_to(jnp.max(top, axis=-1, keepdims=True), top.shape)
+        if kind == "middle":
+            top = top + off
         if kind == "own":
             new = top
         else:
-            old = m_ref[g, :, :, 0:1]
+            old = m_ref[g]
             new = jnp.maximum(old, top)
             alpha = jnp.exp2((old - new) * scale)
-        e = jnp.exp2(s * scale - (new * scale + shift))
-        total = e[:, :, 0:HD]
-        for i in range(1, T // HD):
-            total = total + e[:, :, i * HD : (i + 1) * HD]
-        pv = jnp.dot(
-            e.reshape(R * rows, T).astype(jnp.bfloat16), kv[b, 1, g], preferred_element_type=jnp.float32
-        ).reshape(R, rows, HD)
-        m_ref[g] = jnp.broadcast_to(new, (R, rows, HD))
+        shift = new * scale
+        if kind == "middle":
+            shift = shift - off
+        e = [jnp.exp2(tile * scale - shift) for tile in tiles]
+        total = e[0]
+        for tile in e[1:]:
+            total = total + tile
+        weights = jnp.concatenate([tile.astype(jnp.bfloat16) for tile in e], axis=-1).reshape(R * rows, T)
+        pv = jnp.dot(weights, kv[b, 1, g], preferred_element_type=jnp.float32).reshape(R, rows, HD)
+        m_ref[g] = new
         if kind == "own":
             l_ref[g] = total
             acc_ref[g] = pv

time: 164 us -> 148 us (0.902)
  Pallas kernels: 161 us -> 146 us
    pallas_call x1, Pallas kernels: 161 us -> 146 us  [shards(): pl.pallas_call(functools.partial(kernel, C, H, G, R, T, NP, D), out_shape...]
where the time goes in v2:
time: 148 us
  Pallas kernels  146 us (99%)
  local copies, waits for them, and re-layouts  2.65 us (2%)
    pallas_call x1, Pallas kernels, shards(): pl.pallas_call(functools.partial(kernel, C, H, G, R, T, NP, D), out_shape...  146 us

profile of v2, /device:TPU:6, one launch (start us, length us, event | category | flops | bytes accessed | tf_op | source)
XLA Modules:
  0.0 148.2 jit_solution(17348756610099728273)
XLA Ops:
  0.0 145.6 %shard_map.55 = bf16[96,8192]{1,0:T(8,128)(2,1)} custom-call(s32[16]{0:T(128)} %gate_ref.1, bf16[384,2048]{1,0:T(8,128)(2,1)} %q_ref.1, bf16[384,256]{1,0:T(8,128)(2,1)} %k_ref.1, bf16[384,256]{1,0:T(8,128)(2,1)} %v_ref.1, bf16[2048,8192]{1,0:T(8,128)(2,1)} %w_ref.1), custom_call_target="tpu_custom_call" | custom-call | tf_op jit(solution)/shard_map/pallas_call | solution.py:269
  145.6 2.7 %copy.7 = bf16[96,8192]{1,0:T(8,128)(2,1)} copy(bf16[96,8192]{1,0:T(8,128)(2,1)} %shard_map.55) | data formatting | bytes 3145728

commit v3 on v2

--- a/solution.py
+++ b/solution.py
@@ -29,9 +29,9 @@
 
 def kernel(
     C, H, G, R, T, NP, D,
-    gate_ref, q_ref, k_ref, v_ref, w_ref, out_ref,
-    kv, w, part, ng_ref, m_ref, l_ref, acc_ref, mixed, tmp,
-    w_sem, k_recv, k_send, k_fwd, p_send, p_recv,
+    gate_ref, q_hbm, k_ref, v_ref, w_ref, out_hbm,
+    q_ref, out_ref, kv, w, part, ng_ref, m_ref, l_ref, acc_ref, mixed, tmp,
+    q_sem, kv_sem, out_sem, w_sem, k_recv, k_send, k_fwd, k_relay, p_send, p_recv,
 ):
     c = lax.axis_index("ctx")
     z = lax.axis_index("head")
@@ -44,9 +44,16 @@
     def w_copy(n):
         return pltpu.make_async_copy(w_ref.at[:, pl.ds(n * cols, cols)], w.at[n], w_sem.at[n])
 
+    own_copies = []
     for g in range(G):
-        kv[c, 0, g] = k_ref[:, g * HD : (g + 1) * HD]
-        kv[c, 1, g] = v_ref[:, g * HD : (g + 1) * HD]
+        for i, source in enumerate((k_ref, v_ref)):
+            own_copies.append(
+                pltpu.make_async_copy(source.at[:, pl.ds(g * HD, HD)], kv.at[c, g, i], kv_sem.at[i, g])
+            )
+    q_copy = pltpu.make_async_copy(q_hbm, q_ref, q_sem)
+    for copy in own_copies:
+        copy.start()
+    q_copy.start()
 
     barrier = pltpu.get_barrier_semaphore()
     for q in range(chips):
@@ -66,20 +73,29 @@
     greeted = chips + jnp.where(z > 0, 1, 0) + jnp.where(z < H - 1, 1, 0)
     pl.semaphore_wait(barrier, greeted)
 
-    def kv_copy(block, send, target):
+    for copy in own_copies:
+        copy.wait()
+
+    def kv_copy(block, g, send, target):
         return pltpu.make_async_remote_copy(
-            src_ref=kv.at[block], dst_ref=kv.at[block], send_sem=send, recv_sem=k_recv.at[block],
+            src_ref=kv.at[block, g], dst_ref=kv.at[block, g], send_sem=send.at[g], recv_sem=k_recv.at[block, g],
             device_id={"ctx": target}, device_id_type=MESH,
         )
 
-    for q in reversed(range(chips)):
-        @pl.when(q > p)
+    relays = chips == 4
+
+    def pushes(q):
+        return (q > p) & (q + p != chips - 1) if relays else q > p
+
+    for g in range(G):
+        for q in reversed(range(chips)):
+            @pl.when(pushes(q))
+            def _():
+                kv_copy(c, g, k_send.at[q], 2 * q + k).start()
+
+        @pl.when(k == 0)
         def _():
-            kv_copy(c, k_send.at[q], 2 * q + k).start()
-
-    @pl.when(k == 0)
-    def _():
-        kv_copy(c, k_send.at[p], sibling).start()
+            kv_copy(c, g, k_send.at[p], sibling).start()
 
     for n in range(NP):
         w_copy(n).start()
@@ -88,6 +104,7 @@
         off = jnp.where(gate_ref[h] == 1, 0.0, NEG)
         ng_ref[h] = jnp.full((rows, HD), off, jnp.float32)
 
+    q_copy.wait()
     scale = HD ** -0.5 * LOG2E
 
     def attend(g, r, b, kind):
@@ -96,7 +113,7 @@
             [q_ref[pl.ds(start, rows), (g * R + h) * HD : (g * R + h + 1) * HD] for h in range(R)], axis=0
         )
         s = lax.dot_general(
-            q, kv[b, 0, g], (((1,), (1,)), ((), ())), preferred_element_type=jnp.float32
+            q, kv[b, g, 0], (((1,), (1,)), ((), ())), preferred_element_type=jnp.float32
         ).reshape(R, rows, T)
         tiles = [s[:, :, i * HD : (i + 1) * HD] for i in range(T // HD)]
         off = ng_ref[g * R : (g + 1) * R]
@@ -129,7 +146,7 @@
         for tile in e[1:]:
             total = total + tile
         weights = jnp.concatenate([tile.astype(jnp.bfloat16) for tile in e], axis=-1).reshape(R * rows, T)
-        pv = jnp.dot(weights, kv[b, 1, g], preferred_element_type=jnp.float32).reshape(R, rows, HD)
+        pv = jnp.dot(weights, kv[b, g, 1], preferred_element_type=jnp.float32).reshape(R, rows, HD)
         m_ref[g] = new
         if kind == "own":
             l_ref[g] = total
@@ -139,6 +156,11 @@
             acc_ref[g] = acc_ref[g] * alpha + pv
 
     table = chunk_order(H)
+    relay_target = jnp.where(p == 3, 4, 6) + k
+
+    def out_copy(n):
+        place = pl.ds(pl.multiple_of(n * cols, cols), cols)
+        return pltpu.make_async_copy(out_ref.at[n], out_hbm.at[:, place], out_sem.at[n])
 
     def part_copy(r, n):
         target = jnp.where(r > z, z + 1, z - 1)
@@ -165,16 +187,26 @@
             rest = j - k
             odd = rest % 2
             lead = (k == 1) & (j == 0)
-            b = jnp.where(lead, c - 1, 2 * (p - 1 - rest // 2) + jnp.where(odd == 0, k, 1 - k))
+            turn = rest // 2
+            from_chip = p - 1 - turn
+            if relays:
+                from_chip = jnp.where(p == 2, turn, jnp.where((p == 3) & (turn < 2), 1 + turn, from_chip))
+            b = jnp.where(lead, c - 1, 2 * from_chip + jnp.where(odd == 0, k, 1 - k))
             b = jnp.where(b < 0, 0, b)
 
             @pl.when(step == 0)
             def _():
-                kv_copy(b, k_send.at[0], sibling).wait_recv()
-
-                @pl.when(jnp.logical_not(lead) & (odd == 0))
-                def _():
-                    kv_copy(b, k_fwd.at[b // 2], sibling).start()
+                for g in range(G):
+                    kv_copy(b, g, k_send.at[0], sibling).wait_recv()
+
+                    if relays:
+                        @pl.when(((p == 1 + k) & (b == k)) | ((p == 3) & (b == 2 + k)))
+                        def _():
+                            kv_copy(b, g, k_relay, relay_target).start()
+
+                    @pl.when(jnp.logical_not(lead) & (odd == 0))
+                    def _():
+                        kv_copy(b, g, k_fwd.at[b // 2], sibling).start()
 
             edge = (b == c - 1) | (b == 0)
 
@@ -218,7 +250,8 @@
 
             @pl.when(r == z)
             def _():
-                out_ref[:, pl.ds(pl.multiple_of(n * cols, cols), cols)] = tmp[...].astype(jnp.bfloat16)
+                out_ref[n] = tmp[...].astype(jnp.bfloat16)
+                out_copy(n).start()
 
             @pl.when(r != z)
             def _():
@@ -232,18 +265,24 @@
 
     lax.fori_loop(0, H, chunk, 0)
 
-    for q in range(chips):
-        @pl.when(q > p)
+    for g in range(G):
+        for q in range(chips):
+            @pl.when(pushes(q))
+            def _():
+                kv_copy(c, g, k_send.at[q], 2 * q + k).wait_send()
+
+            @pl.when(q < p)
+            def _():
+                kv_copy(2 * q + k, g, k_fwd.at[q], sibling).wait_send()
+
+        @pl.when(k == 0)
         def _():
-            kv_copy(c, k_send.at[q], 2 * q + k).wait_send()
-
-        @pl.when(q < p)
-        def _():
-            kv_copy(2 * q + k, k_fwd.at[q], sibling).wait_send()
-
-    @pl.when(k == 0)
-    def _():
-        kv_copy(c, k_send.at[p], sibling).wait_send()
+            kv_copy(c, g, k_send.at[p], sibling).wait_send()
+
+        if relays:
+            @pl.when((p == 1 + k) | (p == 3))
+            def _():
+                kv_copy(jnp.where(p == 3, 2 + k, k), g, k_relay, relay_target).wait_send()
 
     def drain(i, carry):
         @pl.when(i // NP != z)
@@ -253,6 +292,8 @@
         return carry
 
     lax.fori_loop(0, H * NP, drain, 0)
+    for n in range(NP):
+        out_copy(n).wait()
 
 
 def solution(mesh):
@@ -265,14 +306,16 @@
         K, D = w_out.shape
         rows = T // H
         NP = 8
-        vmem = pl.BlockSpec(memory_space=pltpu.VMEM)
+        hbm = pl.BlockSpec(memory_space=pl.ANY)
         return pl.pallas_call(
             functools.partial(kernel, C, H, G, R, T, NP, D),
             out_shape=jax.ShapeDtypeStruct((rows, D), jnp.bfloat16),
-            in_specs=[pl.BlockSpec(memory_space=pltpu.SMEM), vmem, vmem, vmem, pl.BlockSpec(memory_space=pl.ANY)],
-            out_specs=vmem,
+            in_specs=[pl.BlockSpec(memory_space=pltpu.SMEM), hbm, hbm, hbm, hbm],
+            out_specs=hbm,
             scratch_shapes=[
-                pltpu.VMEM((C, 2, G, T, HD), jnp.bfloat16),
+                pltpu.VMEM((T, G * R * HD), jnp.bfloat16),
+                pltpu.VMEM((NP, rows, D // NP), jnp.bfloat16),
+                pltpu.VMEM((C, G, 2, T, HD), jnp.bfloat16),
                 pltpu.VMEM((NP, K, D // NP), jnp.bfloat16),
                 pltpu.VMEM((H + 1, NP, rows, D // NP), jnp.bfloat16),
                 pltpu.VMEM((G * R, rows, HD), jnp.float32),
@@ -281,10 +324,14 @@
                 pltpu.VMEM((G, R, rows, HD), jnp.float32),
                 pltpu.VMEM((rows, K), jnp.bfloat16),
                 pltpu.VMEM((rows, D // NP), jnp.float32),
+                pltpu.SemaphoreType.DMA,
+                pltpu.SemaphoreType.DMA((2, G)),
                 pltpu.SemaphoreType.DMA((NP,)),
-                pltpu.SemaphoreType.DMA((C,)),
-                pltpu.SemaphoreType.DMA((C // 2,)),
-                pltpu.SemaphoreType.DMA((C // 2,)),
+                pltpu.SemaphoreType.DMA((NP,)),
+                pltpu.SemaphoreType.DMA((C, G)),
+                pltpu.SemaphoreType.DMA((C // 2, G)),
+                pltpu.SemaphoreType.DMA((C // 2, G)),
+                pltpu.SemaphoreType.DMA((G,)),
                 pltpu.SemaphoreType.DMA((H, NP)),
                 pltpu.SemaphoreType.DMA((H + 1, NP)),
             ],

time: 148 us -> 142 us (0.959)
  Pallas kernels: 146 us -> 139 us
    pallas_call x1, Pallas kernels: 146 us -> 139 us  [shards(): pl.pallas_call(functools.partial(kernel, C, H, G, R, T, NP, D), out_shape...]
where the time goes in v3:
time: 142 us; the launch traced here: 141 us
  Pallas kernels  139 us (98%)
  local copies, waits for them, and re-layouts  2.65 us (2%)
    pallas_call x1, Pallas kernels, shards(): pl.pallas_call(functools.partial(kernel, C, H, G, R, T, NP, D), out_shape...  139 us

profile of v3, /device:TPU:6, one launch (start us, length us, event | category | flops | bytes accessed | tf_op | source)
XLA Modules:
  0.0 141.3 jit_solution(7610614542076697332)
XLA Ops:
  0.0 138.7 %shard_map.55 = bf16[96,8192]{1,0:T(8,128)(2,1)} custom-call(s32[16]{0:T(128)} %gate_ref.1, bf16[384,2048]{1,0:T(8,128)(2,1)} %q_hbm.1, bf16[384,256]{1,0:T(8,128)(2,1)} %k_ref.1, bf16[384,256]{1,0:T(8,128)(2,1)} %v_ref.1, bf16[2048,8192]{1,0:T(8,128)(2,1)} %w_ref.1), custom_call_target="tpu_custom_call" | custom-call | tf_op jit(solution)/shard_map/pallas_call | solution.py:310
  138.7 2.7 %copy.7 = bf16[96,8192]{1,0:T(8,128)(2,1)} copy(bf16[96,8192]{1,0:T(8,128)(2,1)} %shard_map.55) | data formatting | bytes 3145728

commit v4 on v3

--- a/solution.py
+++ b/solution.py
@@ -226,8 +226,18 @@
         for g in range(G):
             o = acc_ref[g] / jnp.sum(l_ref[g], axis=-1, keepdims=True)
             for h in range(R):
-                mixed[:, (g * R + h) * HD : (g * R + h + 1) * HD] = o[h].astype(jnp.bfloat16)
-
+                mixed[step, :, (g * R + h) * HD : (g * R + h + 1) * HD] = o[h].astype(jnp.bfloat16)
+
+        inner_device = (z > 0) & (z < H - 1)
+        ahead_to = jnp.where(step == H - 1, H, jnp.where(step < 2, 0, step))
+        ahead_from = jnp.where(step <= 2, 0, step - 1)
+        first = jnp.where(inner_device, ahead_from, step)
+        last = jnp.where(inner_device, ahead_to, step + 1)
+        lax.fori_loop(first, last, project, 0)
+        return carry
+
+    def project(step, carry):
+        r = pick(table, z, step)
         has_a = ((r > z) & (z > 0)) | ((r < z) & (z < H - 1)) | ((r == z) & (z > 0))
         has_b = (r == z) & (z < H - 1)
 
@@ -236,7 +246,7 @@
             def _():
                 w_copy(n).wait()
 
-            tmp[...] = jnp.dot(mixed[...], w[n], preferred_element_type=jnp.float32)
+            tmp[...] = jnp.dot(mixed[step], w[n], preferred_element_type=jnp.float32)
 
             @pl.when(has_a)
             def _():
@@ -322,7 +332,7 @@
                 pltpu.VMEM((G, R, rows, HD), jnp.float32),
                 pltpu.VMEM((G, R, rows, HD), jnp.float32),
                 pltpu.VMEM((G, R, rows, HD), jnp.float32),
-                pltpu.VMEM((rows, K), jnp.bfloat16),
+                pltpu.VMEM((H, rows, K), jnp.bfloat16),
                 pltpu.VMEM((rows, D // NP), jnp.float32),
                 pltpu.SemaphoreType.DMA,
                 pltpu.SemaphoreType.DMA((2, G)),

time: 142 us -> 142 us (level)
  no operation moved by 1% of the time
where the time goes in v4:
time: 142 us; the launch traced here: 141 us
  Pallas kernels  139 us (98%)
  local copies, waits for them, and re-layouts  2.65 us (2%)
    pallas_call x1, Pallas kernels, shards(): pl.pallas_call(functools.partial(kernel, C, H, G, R, T, NP, D), out_shape...  139 us

profile of v4, /device:TPU:6, one launch (start us, length us, event | category | flops | bytes accessed | tf_op | source)
XLA Modules:
  0.0 141.4 jit_solution(10685435480366026484)
XLA Ops:
  0.0 138.7 %shard_map.55 = bf16[96,8192]{1,0:T(8,128)(2,1)} custom-call(s32[16]{0:T(128)} %gate_ref.1, bf16[384,2048]{1,0:T(8,128)(2,1)} %q_hbm.1, bf16[384,256]{1,0:T(8,128)(2,1)} %k_ref.1, bf16[384,256]{1,0:T(8,128)(2,1)} %v_ref.1, bf16[2048,8192]{1,0:T(8,128)(2,1)} %w_ref.1), custom_call_target="tpu_custom_call" | custom-call | tf_op jit(solution)/shard_map/pallas_call | solution.py:320
  138.7 2.7 %copy.7 = bf16[96,8192]{1,0:T(8,128)(2,1)} copy(bf16[96,8192]{1,0:T(8,128)(2,1)} %shard_map.55) | data formatting | bytes 3145728
